TPU v7x, 512 devices: a whole 4x4x16 slice. The times are simulated.
512 devices in a mesh: slot: 8 (over x, core), tile: 64 (over y, z).
Axes of the slice: x: 4, y: 4, z: 16, core: 2. Of those that a mesh axis runs over, the one named last changes fastest.
Arguments:
- control: float32 [8, 4, 2, 1024, 512], P('slot', None, None, 'tile'), may hold values from -28 to 28
- background: bfloat16 [4, 2, 1024, 512], P(None, None, 'tile'), may hold values from -6 to 6
- self_weight: bfloat16 [512, 512], replicated, may hold values from -0.25 to 0.25
- neighbour_weight: bfloat16 [512, 512], replicated, may hold values from -0.25 to 0.25
- output_weight: bfloat16 [512, 512], replicated, may hold values from -0.25 to 0.25
- norm_gain: float32 [512], replicated, may hold values from 0.1 to 1.9
- readout: bfloat16 [512, 128], replicated, may hold values from -0.25 to 0.25
- error_weight: float32 [512], replicated, may hold values from 0.3 to 3
- report_owner: int32 [8, 2, 8192, 1], P('slot', None, 'tile'), may hold values from 0 to 63, as said below
- report_stencil: int32 [8, 2, 8192, 4], P('slot', None, 'tile'), may hold values from 0 to 31
- report_weights: bfloat16 [8, 2, 8192, 4], P('slot', None, 'tile'), may hold values from 0.049804688 to 1
- report_values: bfloat16 [8, 2, 8192, 128], P('slot', None, 'tile'), may hold values from -6 to 6
- report_precision: bfloat16 [8, 2, 8192], P('slot', None, 'tile'), may hold values from 0.049804688 to 0.5
Outputs:
- gradient: float32 [8, 4, 2, 1024, 512], P('slot', None, None, 'tile')
Inputs may be any that keep to these rules, and one draw needn't show every extreme that they name: `report_owner`: within the rows of one device for one slot and step (aligned blocks of 128 rows) no owner tile is named more than 5 times; in every slot and step one owner tile is named exactly 5 times by every device of the slot. `report_stencil`: A cell of the owner tile, numbered latitude row * 16 + column within the tile.
All inputs are finite; a program needn't handle non-finite values.
Results may differ from a plain program's by a relative error of at most 0.006.
Values may be sent and summed in bfloat16 or wider, within the bound.
A program may use at most 64 MiB of HBM per device.

v0:
```python
import jax
import jax.numpy as jnp
from jax import lax
from jax.sharding import PartitionSpec as P

CAP = 5


EPSILON = 1e-06


def padded_2(cells, sides, width):
    for axis, dim in sides:
        count = lax.axis_size(axis)
        head = lax.slice_in_dim(cells, 0, width, axis=dim)
        tail = lax.slice_in_dim(cells, cells.shape[dim] - width, cells.shape[dim], axis=dim)
        cells = jnp.concatenate(
            [
                lax.ppermute(tail, axis, [(i, (i + 1) % count) for i in range(count)]),
                cells,
                lax.ppermute(head, axis, [((i + 1) % count, i) for i in range(count)]),
            ],
            axis=dim,
        )
    return cells


def shifted(block, axis, distance):
    devices = range(lax.axis_size(axis))
    route = [(i - distance, i) for i in devices if i - distance in devices]
    return lax.ppermute(block, axis, route)


def matmul(operand, matrix):
    flattened = jnp.dot(
        operand.reshape(-1, operand.shape[-1]), matrix, preferred_element_type=jnp.float32
    )
    return flattened.reshape(operand.shape[:-1] + (matrix.shape[-1],))


def matmul_back(operand, matrix):
    flattened = lax.dot_general(
        operand.reshape(-1, operand.shape[-1]),
        matrix,
        (((1,), (1,)), ((), ())),
        preferred_element_type=jnp.float32,
    )
    return flattened.reshape(operand.shape[:-1] + (matrix.shape[0],))


def neighbour_sum(padded):
    widened = padded.astype(jnp.float32)
    centre = widened[:, :, 1:-1, :]
    zero_row = jnp.zeros_like(centre[:, :1])
    northern = jnp.concatenate([zero_row, centre[:, :-1]], axis=1)
    southern = jnp.concatenate([centre[:, 1:], zero_row], axis=1)
    return northern + southern + widened[:, :, :-2, :] + widened[:, :, 2:, :]


def normalize(current, norm_gain):
    inverse_rms = lax.rsqrt(jnp.mean(current * current, axis=-1, keepdims=True) + EPSILON)
    return ((current * inverse_rms * norm_gain).astype(jnp.bfloat16), inverse_rms)


def pre_activation(current, norm_gain, self_weight, neighbour_weight):
    normed, inverse_rms = normalize(current, norm_gain)
    padded = padded_2(normed, (("tile", 2),), 1)
    mixed_mean = (0.25 * neighbour_sum(padded)).astype(jnp.bfloat16)
    return (inverse_rms, matmul(normed, self_weight) + matmul(mixed_mean, neighbour_weight))


def adjoint(
    current,
    inverse_rms,
    linear_sum,
    cotangent,
    norm_gain,
    self_weight,
    neighbour_weight,
    output_weight,
):
    grad_active = matmul_back(cotangent.astype(jnp.bfloat16), output_weight)
    sigmoid_value = jax.nn.sigmoid(linear_sum)
    grad_input = (grad_active * sigmoid_value * (1.0 + linear_sum * (1.0 - sigmoid_value))).astype(
        jnp.bfloat16
    )
    grad_mixed = matmul_back(grad_input, neighbour_weight).astype(jnp.bfloat16)
    padded = padded_2(grad_mixed, (("tile", 2),), 1)
    grad_normed = matmul_back(grad_input, self_weight) + 0.25 * neighbour_sum(padded)
    scaled = norm_gain * grad_normed
    cubed_rms = inverse_rms * inverse_rms * inverse_rms
    return (
        cotangent
        + inverse_rms * scaled
        - current * cubed_rms * jnp.mean(current * scaled, axis=-1, keepdims=True)
    )


def observe(current, arrived_values, arrived_weights, arrived_precision, arrived_stencil, readout):
    members, lat_rows, lon_cols, channels = current.shape
    cell_count = lat_rows * lon_cols
    readout_field = jnp.dot(
        current.astype(jnp.bfloat16).reshape(-1, channels),
        readout,
        preferred_element_type=jnp.float32,
    )
    readout_field = readout_field.reshape(members, cell_count, readout.shape[1])
    stencil_weights = arrived_weights.astype(jnp.float32)
    scaling = arrived_precision.astype(jnp.float32)[None, :, None]
    targets = arrived_values.astype(jnp.float32)[None]
    cell_hits = (
        arrived_stencil[:, :, None] == jnp.arange(cell_count, dtype=jnp.int32)[None, None, :]
    )
    weight_table = jnp.sum(jnp.where(cell_hits, stencil_weights[:, :, None], 0.0), axis=1)
    picked = readout_field[:, arrived_stencil, :]
    predicted = jnp.sum(picked * stencil_weights[None, :, :, None], axis=2)
    misfit = scaling * (predicted - targets)
    spread = jnp.einsum(
        "rc,mro->mco",
        weight_table,
        misfit,
        precision=lax.Precision.HIGHEST,
        preferred_element_type=jnp.float32,
    )
    pulled = matmul_back(spread.astype(jnp.bfloat16), readout)
    return pulled.reshape(current.shape)


def per_device(
    control,
    background,
    self_weight,
    neighbour_weight,
    output_weight,
    norm_gain,
    readout,
    error_weight,
    report_owner,
    report_stencil,
    report_weights,
    report_values,
    report_precision,
):
    tile_count = lax.axis_size("tile")
    slot_index = lax.axis_index("slot")
    owners = report_owner[0, :, :, 0]
    step_count = owners.shape[0]
    row_count = owners.shape[1]
    owner_hits = (
        owners[:, :, None] == jnp.arange(tile_count, dtype=jnp.int32)[None, None, :]
    ).astype(jnp.float32)
    row_ids = jnp.arange(row_count, dtype=jnp.int32)
    earlier_rows = (row_ids[:, None] > row_ids[None, :]).astype(jnp.float32)
    earlier_counts = jnp.einsum(
        "rq,kqt->krt",
        earlier_rows,
        owner_hits,
        precision=lax.Precision.HIGHEST,
        preferred_element_type=jnp.float32,
    )
    owner_rank = jnp.sum(earlier_counts * owner_hits, axis=2).astype(jnp.int32)
    destination = owners * CAP + owner_rank
    slot_total = tile_count * CAP
    placement = destination[:, None, :] == jnp.arange(slot_total, dtype=jnp.int32)[None, :, None]
    placement16 = placement.astype(jnp.bfloat16)

    def bucket_float(entries):
        placed = jnp.einsum(
            "ksr,kr...->ks...", placement16, entries, preferred_element_type=jnp.float32
        ).astype(entries.dtype)
        return placed.reshape((step_count, tile_count, CAP) + entries.shape[2:])

    placed_stencil = jnp.sum(
        jnp.where(placement[:, :, :, None], report_stencil[0][:, None, :, :], 0), axis=2
    )
    placed_stencil = placed_stencil.reshape((step_count, tile_count, CAP, report_stencil.shape[3]))
    arrived = (
        lax.all_to_all(
            bucket_float(report_values[0]), "tile", split_axis=1, concat_axis=1, tiled=True
        ),
        lax.all_to_all(
            bucket_float(report_weights[0]), "tile", split_axis=1, concat_axis=1, tiled=True
        ),
        lax.all_to_all(
            bucket_float(report_precision[0]), "tile", split_axis=1, concat_axis=1, tiled=True
        ),
        lax.all_to_all(placed_stencil, "tile", split_axis=1, concat_axis=1, tiled=True),
    )
    arrived_values, arrived_weights, arrived_precision, arrived_stencil = [
        received.reshape((step_count, tile_count * CAP) + received.shape[3:])
        for received in arrived
    ]
    current = control[0]
    states = [current]
    kept = []
    for step_index in range(step_count):
        inverse_rms, linear_sum = pre_activation(current, norm_gain, self_weight, neighbour_weight)
        kept.append((inverse_rms, linear_sum))
        current = current + matmul(jax.nn.silu(linear_sum).astype(jnp.bfloat16), output_weight)
        states.append(current)
    final_state = current.astype(jnp.bfloat16)
    arrived_final = shifted(final_state, "slot", 1)
    previous = jnp.where(slot_index == 0, background, arrived_final).astype(jnp.float32)
    model_misfit = error_weight * (states[0] - previous)
    pulls = [
        observe(
            states[step_index + 1],
            arrived_values[step_index],
            arrived_weights[step_index],
            arrived_precision[step_index],
            arrived_stencil[step_index],
            readout,
        )
        for step_index in range(step_count)
    ]
    next_misfit = shifted(model_misfit.astype(jnp.bfloat16), "slot", -1).astype(model_misfit.dtype)
    cotangent = pulls[step_count - 1] - next_misfit
    for step_index in reversed(range(step_count)):
        inverse_rms, linear_sum = pre_activation(
            states[step_index], norm_gain, self_weight, neighbour_weight
        )
        cotangent = adjoint(
            states[step_index],
            inverse_rms,
            linear_sum,
            cotangent,
            norm_gain,
            self_weight,
            neighbour_weight,
            output_weight,
        )
        if step_index > 0:
            cotangent = cotangent + pulls[step_index - 1]
    return (cotangent + model_misfit)[None]


def solution(mesh):
    in_specs = (
        P("slot", None, None, "tile", None),
        P(None, None, "tile", None),
        P(),
        P(),
        P(),
        P(),
        P(),
        P(),
        P("slot", None, "tile", None),
        P("slot", None, "tile", None),
        P("slot", None, "tile", None),
        P("slot", None, "tile", None),
        P("slot", None, "tile"),
    )
    out_specs = P("slot", None, None, "tile", None)
    return jax.shard_map(
        per_device, mesh=mesh, in_specs=in_specs, out_specs=out_specs, check_vma=False
    )
```

profile of v0, /device:TPU:6, one launch (start us, length us, event | category | flops | bytes accessed | tf_op | source)
XLA Modules:
  0.0 169.3 jit_solution(3656091437307377876)
XLA Ops:
  0.0 1.1 fusion.31
  1.1 0.6 multiply_multiply_fusion
  1.7 1.1 fusion.33
  2.9 3.8 %collective-permute-start = (bf16[4,2,1,512]{3,2,1,0:T(2,128)(2,1)S(1)}, bf16[4,2,1,512]{3,2,1,0:T(2,128)(2,1)S(1)}, u32[]{:S(2)}, u32[]{:S(2)}) collective-permute-start(bf16[4,2,1,512]{3,2,1,0:T(2,128)(2,1)S(1)} %get-tuple-element.29), channel_id=1, source_target_pairs={{0,1},{1,2},{2,3},{3,4},{4,5},{5,6},{6,7},{7,8},{8,9},{9,10},{10,1... | collective-permute-start | bytes 24584 | tf_op jit(solution)/shard_map/ppermute | solution.py:19
  6.7 11.9 %collective-permute-start.1 = (bf16[4,2,1,512]{3,2,1,0:T(2,128)(2,1)S(1)}, bf16[4,2,1,512]{3,2,1,0:T(2,128)(2,1)S(1)}, u32[]{:S(2)}, u32[]{:S(2)}) collective-permute-start(bf16[4,2,1,512]{3,2,1,0:T(2,128)(2,1)S(1)} %get-tuple-element.30), channel_id=1, source_target_pairs={{1,0},{2,1},{3,2},{4,3},{5,4},{6,5},{7,6},{8,7},{9,8},{10,9},{11,1... | collective-permute-start | bytes 24584 | tf_op jit(solution)/shard_map/ppermute | solution.py:21
  18.7 0.9 fusion.8
  19.6 0.7 convert_add_fusion
  20.3 0.8 fusion.41
  21.3 0.7 copy.72
  21.9 10.0 %all-to-all-start = ((bf16[2,64,5]{2,0,1:T(2,128)(2,1)}), bf16[2,64,5]{2,0,1:T(2,128)(2,1)S(1)}, u32[]{:S(2)}, u32[]{:S(2)}) async-start(bf16[2,64,5]{2,0,1:T(2,128)(2,1)} %copy.72), calls=%async_computation | async-start | bytes 65536 | tf_op jit(solution)/shard_map/all_to_all | solution.py:184
  32.0 0.2 fusion.23
  32.3 0.9 convolution_convert_fusion.5
  33.2 1.0 convolution_convert_fusion
  34.2 1.2 select_reduce_fusion
  35.6 0.9 copy.73
  36.5 0.2 reshape.281
  36.7 0.8 copy.77
  37.5 0.8 copy.81
  38.3 8.0 %all-to-all-done = bf16[2,64,5]{2,0,1:T(2,128)(2,1)S(1)} async-done(((bf16[2,64,5]{2,0,1:T(2,128)(2,1)}), bf16[2,64,5]{2,0,1:T(2,128)(2,1)S(1)}, u32[]{:S(2)}, u32[]{:S(2)}) %all-to-all-start) | async-done | bytes 1312 | tf_op jit(solution)/shard_map/all_to_all | solution.py:184
  46.3 7.1 %all-to-all-start.2 = ((bf16[2,64,5,4]{2,3,0,1:T(4,128)(2,1)}), bf16[2,64,5,4]{2,3,0,1:T(4,128)(2,1)S(1)}, u32[]{:S(2)}, u32[]{:S(2)}) async-start(bf16[2,64,5,4]{2,3,0,1:T(4,128)(2,1)} %copy.77), calls=%async_computation.2 | async-start | bytes 262144 | tf_op jit(solution)/shard_map/all_to_all | solution.py:181
  53.8 0.7 reshape.286
  54.7 0.2 convolution_add_fusion.5
  55.0 0.3 multiply_reduce_fusion.3
  55.3 0.6 multiply_multiply_fusion.1
  56.1 3.5 %collective-permute-start.2 = (bf16[4,2,1,512]{3,2,1,0:T(2,128)(2,1)S(1)}, bf16[4,2,1,512]{3,2,1,0:T(2,128)(2,1)S(1)}, u32[]{:S(2)}, u32[]{:S(2)}) collective-permute-start(bf16[4,2,1,512]{3,2,1,0:T(2,128)(2,1)S(1)} %get-tuple-element.27), channel_id=1, source_target_pairs={{0,1},{1,2},{2,3},{3,4},{4,5},{5,6},{6,7},{7,8},{8,9},{9,10},{10,1... | collective-permute-start | bytes 24584 | tf_op jit(solution)/shard_map/ppermute | solution.py:19
  59.6 5.8 %collective-permute-start.3 = (bf16[4,2,1,512]{3,2,1,0:T(2,128)(2,1)S(1)}, bf16[4,2,1,512]{3,2,1,0:T(2,128)(2,1)S(1)}, u32[]{:S(2)}, u32[]{:S(2)}) collective-permute-start(bf16[4,2,1,512]{3,2,1,0:T(2,128)(2,1)S(1)} %get-tuple-element.28), channel_id=1, source_target_pairs={{1,0},{2,1},{3,2},{4,3},{5,4},{6,5},{7,6},{8,7},{9,8},{10,9},{11,1... | collective-permute-start | bytes 24584 | tf_op jit(solution)/shard_map/ppermute | solution.py:21
  65.4 0.2 fusion.21
  65.7 1.2 collective-permute-done.3
  67.0 0.2 convolution_add_fusion.3
  67.2 0.9 fusion.4
  68.1 1.9 %collective-permute-start.4 = (bf16[4,2,16,512]{3,2,1,0:T(8,128)(2,1)}, bf16[4,2,16,512]{3,2,1,0:T(8,128)(2,1)}, u32[]{:S(2)}, u32[]{:S(2)}) collective-permute-start(bf16[4,2,16,512]{3,2,1,0:T(8,128)(2,1)} %fusion.4), channel_id=1, source_target_pairs={{0,64},{64,128},{128,192},{192,256},{256,320},{320,384},{384,448},... | collective-permute-start | bytes 393224 | tf_op jit(solution)/shard_map/ppermute | solution.py:31
  70.1 1.1 fusion.57
  71.2 13.9 %all-to-all-start.1 = ((s32[2,64,5,4]{2,3,0,1:T(4,128)}), s32[2,64,5,4]{2,3,0,1:T(4,128)S(1)}, u32[]{:S(2)}, u32[]{:S(2)}) async-start(s32[2,64,5,4]{2,3,0,1:T(4,128)} %copy.73), calls=%async_computation.1 | async-start | bytes 524288 | tf_op jit(solution)/shard_map/all_to_all | solution.py:187
  85.5 0.8 copy.80
  86.8 0.8 copy.89
  87.6 14.7 %all-to-all-done.1 = s32[2,64,5,4]{2,3,0,1:T(4,128)S(1)} async-done(((s32[2,64,5,4]{2,3,0,1:T(4,128)}), s32[2,64,5,4]{2,3,0,1:T(4,128)S(1)}, u32[]{:S(2)}, u32[]{:S(2)}) %all-to-all-start.1) | async-done | bytes 10272 | tf_op jit(solution)/shard_map/all_to_all | solution.py:187
  102.3 6.9 %all-to-all-start.3 = ((bf16[2,64,5,128]{3,0,2,1:T(2,128)(2,1)}), bf16[2,64,5,128]{3,0,2,1:T(2,128)(2,1)}, u32[]{:S(2)}, u32[]{:S(2)}) async-start(bf16[2,64,5,128]{3,0,2,1:T(2,128)(2,1)} %bitcast.22), calls=%async_computation.3 | async-start | bytes 327680 | tf_op jit(solution)/shard_map/all_to_all | solution.py:178
  109.9 0.6 copy-done.11
  110.6 4.3 %gather_fusion = f32[1280,4,128]{2,1,0:T(4,128)S(1)} fusion(f32[4,32,128]{2,0,1:T(4,128)S(1)} %copy.76, s32[2048]{0:T(1024)S(1)} %pad_clamp_fusion.1), kind=kCustom, calls=%fused_computation | custom fusion | bytes 5248000 | tf_op jit(solution)/shard_map/gather | solution.py:115
  115.0 3.9 %multiply_reduce_fusion.1 = f32[320,4,128]{2,1,0:T(4,128)} fusion(f32[320,4,4,128]{3,2,1,0:T(4,128)S(1)} %bitcast.171, f32[320,4]{1,0:T(8,128)} %copy.80), kind=kLoop, calls=%fused_computation.3 | loop fusion | flops 1146880 | bytes 3281920 | tf_op jit(solution)/shard_map/reduce_sum | solution.py:116
  118.9 1.1 eq.74
  120.4 0.6 select_reduce_fusion.1
  121.0 1.0 fusion.40
  122.0 7.3 %collective-permute-start.5 = (bf16[4,2,16,512]{3,2,1,0:T(8,128)(2,1)S(1)}, bf16[4,2,16,512]{3,2,1,0:T(8,128)(2,1)S(1)}, u32[]{:S(2)}, u32[]{:S(2)}) collective-permute-start(bf16[4,2,16,512]{3,2,1,0:T(8,128)(2,1)S(1)} %fusion.40), channel_id=1, source_target_pairs={{64,0},{128,64},{192,128},{256,192},{320,256},{384,320},{448,384},... | collective-permute-start | bytes 393224 | tf_op jit(solution)/shard_map/ppermute | solution.py:31
  129.3 2.0 %slice_convert_fusion = (f32[1,64,5,128]{3,0,2,1:T(1,128)}, f32[1,64,5,128]{3,0,2,1:T(1,128)S(1)}) fusion(bf16[2,64,5,128]{3,0,2,1:T(2,128)(2,1)} %all-to-all-done.3), kind=kLoop, calls=%fused_computation.96 | loop fusion | flops 81920 | bytes 491520 | tf_op jit(solution)/shard_map/convert_element_type | solution.py:110
  131.3 1.5 multiply_bitcast_fusion.1
  132.8 0.5 convolution_convert_fusion.4
  133.6 0.3 fusion.6
  133.9 0.3 convolution_convert_fusion.2
  134.2 3.1 %collective-permute-start.6 = (bf16[4,2,1,512]{3,2,1,0:T(2,128)(2,1)S(1)}, bf16[4,2,1,512]{3,2,1,0:T(2,128)(2,1)S(1)}, u32[]{:S(2)}, u32[]{:S(2)}) collective-permute-start(bf16[4,2,1,512]{3,2,1,0:T(2,128)(2,1)S(1)} %get-tuple-element.25), channel_id=1, source_target_pairs={{0,1},{1,2},{2,3},{3,4},{4,5},{5,6},{6,7},{7,8},{8,9},{9,10},{10,1... | collective-permute-start | bytes 24584 | tf_op jit(solution)/shard_map/ppermute | solution.py:19
  137.4 6.0 %collective-permute-start.7 = (bf16[4,2,1,512]{3,2,1,0:T(2,128)(2,1)S(1)}, bf16[4,2,1,512]{3,2,1,0:T(2,128)(2,1)S(1)}, u32[]{:S(2)}, u32[]{:S(2)}) collective-permute-start(bf16[4,2,1,512]{3,2,1,0:T(2,128)(2,1)S(1)} %get-tuple-element.26), channel_id=1, source_target_pairs={{1,0},{2,1},{3,2},{4,3},{5,4},{6,5},{7,6},{8,7},{9,8},{10,9},{11,1... | collective-permute-start | bytes 24584 | tf_op jit(solution)/shard_map/ppermute | solution.py:21
  143.5 1.4 collective-permute-done.7
  145.0 1.0 multiply_reduce_fusion.2
  146.2 4.3 %gather_fusion.1 = f32[1280,4,128]{2,1,0:T(4,128)S(1)} fusion(f32[4,32,128]{2,0,1:T(4,128)S(1)} %copy.86, s32[2048]{0:T(1024)S(1)} %pad_clamp_fusion), kind=kCustom, calls=%fused_computation.1 | custom fusion | bytes 5248000 | tf_op jit(solution)/shard_map/gather | solution.py:115
  150.7 3.2 %multiply_reduce_fusion = f32[320,4,128]{2,1,0:T(4,128)S(1)} fusion(f32[320,4,4,128]{3,2,1,0:T(4,128)S(1)} %bitcast.172, f32[320,4]{1,0:T(8,128)} %copy.89), kind=kLoop, calls=%fused_computation.2 | loop fusion | flops 1146880 | bytes 3281920 | tf_op jit(solution)/shard_map/reduce_sum | solution.py:116
  154.0 0.6 multiply_bitcast_fusion
  154.6 0.5 convolution_convert_fusion.3
  155.4 0.3 fusion.5
  155.7 0.3 convolution_convert_fusion.1
  156.1 1.9 %collective-permute-start.8 = (bf16[4,2,1,512]{3,2,1,0:T(2,128)(2,1)S(1)}, bf16[4,2,1,512]{3,2,1,0:T(2,128)(2,1)S(1)}, u32[]{:S(2)}, u32[]{:S(2)}) collective-permute-start(bf16[4,2,1,512]{3,2,1,0:T(2,128)(2,1)S(1)} %get-tuple-element.21), channel_id=1, source_target_pairs={{0,1},{1,2},{2,3},{3,4},{4,5},{5,6},{6,7},{7,8},{8,9},{9,10},{10,1... | collective-permute-start | bytes 24584 | tf_op jit(solution)/shard_map/ppermute | solution.py:19
  158.0 7.5 %collective-permute-start.9 = (bf16[4,2,1,512]{3,2,1,0:T(2,128)(2,1)S(1)}, bf16[4,2,1,512]{3,2,1,0:T(2,128)(2,1)S(1)}, u32[]{:S(2)}, u32[]{:S(2)}) collective-permute-start(bf16[4,2,1,512]{3,2,1,0:T(2,128)(2,1)S(1)} %get-tuple-element.22), channel_id=1, source_target_pairs={{1,0},{2,1},{3,2},{4,3},{5,4},{6,5},{7,6},{8,7},{9,8},{10,9},{11,1... | collective-permute-start | bytes 24584 | tf_op jit(solution)/shard_map/ppermute | solution.py:21
  165.6 1.4 collective-permute-done.9
  167.1 0.4 fusion.39
  167.5 1.8 %fusion.38 = f32[1,4,2,16,512]{4,3,2,1,0:T(8,128)} fusion(f32[1,4,2,16,512]{4,3,2,1,0:T(8,128)S(1)} %copy-done.4, f32[4,2,16,512]{3,2,1,0:T(8,128)S(1)} %subtract_add_fusion, f32[4,2,16,512]{3,2,1,0:T(8,128)S(1)} %get-tuple-element.39, f32[4,2,16]{2,1,0:T(2,128)S(1)} %broadcast_multiply_fusion, f32[4,2,16]{2,1,0:T(2,128)S(1)} %copy-done.26, ...), kind=kLoop, calls=%fused_computation.74 | loop fusion | flops 655360 | bytes 1314305 | tf_op jit(solution)/shard_map/broadcast_in_dim | solution.py:234
  (124 shorter events, 4.1 us)
Async XLA Ops:
  0.0 32.0 %copy-start = (bf16[512,512]{1,0:T(8,128)(2,1)S(1)}, bf16[512,512]{1,0:T(8,128)(2,1)}, u32[]{:S(2)}) copy-start(bf16[512,512]{1,0:T(8,128)(2,1)} %param.15) | copy-start | bytes 1572868
  1.7 53.0 %copy-start.1 = (bf16[512,512]{1,0:T(8,128)(2,1)S(1)}, bf16[512,512]{1,0:T(8,128)(2,1)}, u32[]{:S(2)}) copy-start(bf16[512,512]{1,0:T(8,128)(2,1)} %param.16) | copy-start | bytes 1572868
  2.9 51.7 %collective-permute-start = (bf16[4,2,1,512]{3,2,1,0:T(2,128)(2,1)S(1)}, bf16[4,2,1,512]{3,2,1,0:T(2,128)(2,1)S(1)}, u32[]{:S(2)}, u32[]{:S(2)}) collective-permute-start(bf16[4,2,1,512]{3,2,1,0:T(2,128)(2,1)S(1)} %get-tuple-element.29), channel_id=1, source_target_pairs={{0,1},{1,2},{2,3},{3,4},{4,5},{5,6},{6,7},{7,8},{8,9},{9,10},{10,1... | collective-permute-start | bytes 24584 | tf_op jit(solution)/shard_map/ppermute | solution.py:19
  6.7 47.9 %collective-permute-start.1 = (bf16[4,2,1,512]{3,2,1,0:T(2,128)(2,1)S(1)}, bf16[4,2,1,512]{3,2,1,0:T(2,128)(2,1)S(1)}, u32[]{:S(2)}, u32[]{:S(2)}) collective-permute-start(bf16[4,2,1,512]{3,2,1,0:T(2,128)(2,1)S(1)} %get-tuple-element.30), channel_id=1, source_target_pairs={{1,0},{2,1},{3,2},{4,3},{5,4},{6,5},{7,6},{8,7},{9,8},{10,9},{11,1... | collective-permute-start | bytes 24584 | tf_op jit(solution)/shard_map/ppermute | solution.py:21
  21.9 24.4 %all-to-all-start = ((bf16[2,64,5]{2,0,1:T(2,128)(2,1)}), bf16[2,64,5]{2,0,1:T(2,128)(2,1)S(1)}, u32[]{:S(2)}, u32[]{:S(2)}) async-start(bf16[2,64,5]{2,0,1:T(2,128)(2,1)} %copy.72), calls=%async_computation | async-start | bytes 65536 | tf_op jit(solution)/shard_map/all_to_all | solution.py:184
  32.2 22.7 %copy-start.4 = (f32[1,4,2,16,512]{4,3,2,1,0:T(8,128)S(1)}, f32[1,4,2,16,512]{4,3,2,1,0:T(8,128)}, u32[]{:S(2)}) copy-start(f32[1,4,2,16,512]{4,3,2,1,0:T(8,128)} %param.13) | copy-start | bytes 786436
  32.3 22.7 %copy-start.31 = (bf16[512,512]{1,0:T(8,128)(2,1)S(1)}, bf16[512,512]{1,0:T(8,128)(2,1)}, u32[]{:S(2)}) copy-start(bf16[512,512]{1,0:T(8,128)(2,1)} %param.17) | copy-start | bytes 1572868
  37.5 18.5 %copy-start.24 = (f32[512]{0:T(512)S(1)}, f32[512]{0:T(512)}, u32[]{:S(2)}) copy-start(f32[512]{0:T(512)} %param.18) | copy-start | bytes 6148
  46.3 24.9 %all-to-all-start.2 = ((bf16[2,64,5,4]{2,3,0,1:T(4,128)(2,1)}), bf16[2,64,5,4]{2,3,0,1:T(4,128)(2,1)S(1)}, u32[]{:S(2)}, u32[]{:S(2)}) async-start(bf16[2,64,5,4]{2,3,0,1:T(4,128)(2,1)} %copy.77), calls=%async_computation.2 | async-start | bytes 262144 | tf_op jit(solution)/shard_map/all_to_all | solution.py:181
  55.0 4.6 %copy-start.17 = (f32[4,2,16,512]{3,2,1,0:T(8,128)}, f32[4,2,16,512]{3,2,1,0:T(8,128)S(1)}, u32[]{:S(2)}) copy-start(f32[4,2,16,512]{3,2,1,0:T(8,128)S(1)} %convolution_add_fusion.5) | copy-start | bytes 786436
  55.3 12.8 %copy-start.5 = (f32[4,2,16,512]{3,2,1,0:T(8,128)}, f32[4,2,16,512]{3,2,1,0:T(8,128)S(1)}, u32[]{:S(2)}) copy-start(f32[4,2,16,512]{3,2,1,0:T(8,128)S(1)} %get-tuple-element.36) | copy-start | bytes 786436
  56.1 9.6 %collective-permute-start.2 = (bf16[4,2,1,512]{3,2,1,0:T(2,128)(2,1)S(1)}, bf16[4,2,1,512]{3,2,1,0:T(2,128)(2,1)S(1)}, u32[]{:S(2)}, u32[]{:S(2)}) collective-permute-start(bf16[4,2,1,512]{3,2,1,0:T(2,128)(2,1)S(1)} %get-tuple-element.27), channel_id=1, source_target_pairs={{0,1},{1,2},{2,3},{3,4},{4,5},{5,6},{6,7},{7,8},{8,9},{9,10},{10,1... | collective-permute-start | bytes 24584 | tf_op jit(solution)/shard_map/ppermute | solution.py:19
  59.6 10.5 %copy-start.8 = (bf16[512,128]{1,0:T(8,128)(2,1)S(1)}, bf16[512,128]{1,0:T(8,128)(2,1)}, u32[]{:S(2)}) copy-start(bf16[512,128]{1,0:T(8,128)(2,1)} %param.19) | copy-start | bytes 393220
  59.6 7.2 %collective-permute-start.3 = (bf16[4,2,1,512]{3,2,1,0:T(2,128)(2,1)S(1)}, bf16[4,2,1,512]{3,2,1,0:T(2,128)(2,1)S(1)}, u32[]{:S(2)}, u32[]{:S(2)}) collective-permute-start(bf16[4,2,1,512]{3,2,1,0:T(2,128)(2,1)S(1)} %get-tuple-element.28), channel_id=1, source_target_pairs={{1,0},{2,1},{3,2},{4,3},{5,4},{6,5},{7,6},{8,7},{9,8},{10,9},{11,1... | collective-permute-start | bytes 24584 | tf_op jit(solution)/shard_map/ppermute | solution.py:21
  67.2 3.9 %copy-start.19 = (f32[4,2,16,512]{3,2,1,0:T(8,128)}, f32[4,2,16,512]{3,2,1,0:T(8,128)S(1)}, u32[]{:S(2)}) copy-start(f32[4,2,16,512]{3,2,1,0:T(8,128)S(1)} %convolution_add_fusion.3) | copy-start | bytes 786436
  68.1 52.9 %collective-permute-start.4 = (bf16[4,2,16,512]{3,2,1,0:T(8,128)(2,1)}, bf16[4,2,16,512]{3,2,1,0:T(8,128)(2,1)}, u32[]{:S(2)}, u32[]{:S(2)}) collective-permute-start(bf16[4,2,16,512]{3,2,1,0:T(8,128)(2,1)} %fusion.4), channel_id=1, source_target_pairs={{0,64},{64,128},{128,192},{192,256},{256,320},{320,384},{384,448},... | collective-permute-start | bytes 393224 | tf_op jit(solution)/shard_map/ppermute | solution.py:31
  71.2 31.1 %all-to-all-start.1 = ((s32[2,64,5,4]{2,3,0,1:T(4,128)}), s32[2,64,5,4]{2,3,0,1:T(4,128)S(1)}, u32[]{:S(2)}, u32[]{:S(2)}) async-start(s32[2,64,5,4]{2,3,0,1:T(4,128)} %copy.73), calls=%async_computation.1 | async-start | bytes 524288 | tf_op jit(solution)/shard_map/all_to_all | solution.py:187
  102.3 27.0 %all-to-all-start.3 = ((bf16[2,64,5,128]{3,0,2,1:T(2,128)(2,1)}), bf16[2,64,5,128]{3,0,2,1:T(2,128)(2,1)}, u32[]{:S(2)}, u32[]{:S(2)}) async-start(bf16[2,64,5,128]{3,0,2,1:T(2,128)(2,1)} %bitcast.22), calls=%async_computation.3 | async-start | bytes 327680 | tf_op jit(solution)/shard_map/all_to_all | solution.py:178
  109.9 0.6 copy-start.11
  115.0 6.0 %copy-start.28 = (f32[512]{0:T(512)S(1)}, f32[512]{0:T(512)}, u32[]{:S(2)}) copy-start(f32[512]{0:T(512)} %param.20) | copy-start | bytes 6148
  118.9 14.4 %copy-start.9 = (bf16[512,128]{1,0:T(8,128)(2,1)S(1)}, bf16[512,128]{1,0:T(8,128)(2,1)}, u32[]{:S(2)}) copy-start(bf16[512,128]{1,0:T(8,128)(2,1)} %param.19) | copy-start | bytes 393220
  118.9 14.6 %copy-start.20 = (f32[4,2,16,512]{3,2,1,0:T(8,128)S(1)}, f32[4,2,16,512]{3,2,1,0:T(8,128)}, u32[]{:S(2)}) copy-start(f32[4,2,16,512]{3,2,1,0:T(8,128)} %copy-done.19) | copy-start | bytes 786436
  118.9 14.6 %copy-start.32 = (bf16[512,512]{1,0:T(8,128)(2,1)S(1)}, bf16[512,512]{1,0:T(8,128)(2,1)}, u32[]{:S(2)}) copy-start(bf16[512,512]{1,0:T(8,128)(2,1)} %param.17) | copy-start | bytes 1572868
  122.0 11.9 %copy-start.2 = (bf16[512,512]{1,0:T(8,128)(2,1)S(1)}, bf16[512,512]{1,0:T(8,128)(2,1)}, u32[]{:S(2)}) copy-start(bf16[512,512]{1,0:T(8,128)(2,1)} %param.16) | copy-start | bytes 1572868
  122.0 11.5 %collective-permute-start.5 = (bf16[4,2,16,512]{3,2,1,0:T(8,128)(2,1)S(1)}, bf16[4,2,16,512]{3,2,1,0:T(8,128)(2,1)S(1)}, u32[]{:S(2)}, u32[]{:S(2)}) collective-permute-start(bf16[4,2,16,512]{3,2,1,0:T(8,128)(2,1)S(1)} %fusion.40), channel_id=1, source_target_pairs={{64,0},{128,64},{192,128},{256,192},{320,256},{384,320},{448,384},... | collective-permute-start | bytes 393224 | tf_op jit(solution)/shard_map/ppermute | solution.py:31
  132.8 12.2 %copy-start.6 = (f32[4,2,16,512]{3,2,1,0:T(8,128)S(1)}, f32[4,2,16,512]{3,2,1,0:T(8,128)}, u32[]{:S(2)}) copy-start(f32[4,2,16,512]{3,2,1,0:T(8,128)} %copy-done.5) | copy-start | bytes 786436
  133.5 9.9 %copy-start.12 = (f32[4,2,16,512]{3,2,1,0:T(8,128)}, f32[4,2,16,512]{3,2,1,0:T(8,128)S(1)}, u32[]{:S(2)}) copy-start(f32[4,2,16,512]{3,2,1,0:T(8,128)S(1)} %fusion.51) | copy-start | bytes 786436
  133.5 12.4 %copy-start.22 = (bf16[4,2,16,512]{3,2,1,0:T(8,128)(2,1)}, bf16[4,2,16,512]{3,2,1,0:T(8,128)(2,1)S(1)}, u32[]{:S(2)}) copy-start(bf16[4,2,16,512]{3,2,1,0:T(8,128)(2,1)S(1)} %collective-permute-done.5) | copy-start | bytes 393220
  134.2 9.2 %collective-permute-start.6 = (bf16[4,2,1,512]{3,2,1,0:T(2,128)(2,1)S(1)}, bf16[4,2,1,512]{3,2,1,0:T(2,128)(2,1)S(1)}, u32[]{:S(2)}, u32[]{:S(2)}) collective-permute-start(bf16[4,2,1,512]{3,2,1,0:T(2,128)(2,1)S(1)} %get-tuple-element.25), channel_id=1, source_target_pairs={{0,1},{1,2},{2,3},{3,4},{4,5},{5,6},{6,7},{7,8},{8,9},{9,10},{10,1... | collective-permute-start | bytes 24584 | tf_op jit(solution)/shard_map/ppermute | solution.py:19
  137.4 7.5 %collective-permute-start.7 = (bf16[4,2,1,512]{3,2,1,0:T(2,128)(2,1)S(1)}, bf16[4,2,1,512]{3,2,1,0:T(2,128)(2,1)S(1)}, u32[]{:S(2)}, u32[]{:S(2)}) collective-permute-start(bf16[4,2,1,512]{3,2,1,0:T(2,128)(2,1)S(1)} %get-tuple-element.26), channel_id=1, source_target_pairs={{1,0},{2,1},{3,2},{4,3},{5,4},{6,5},{7,6},{8,7},{9,8},{10,9},{11,1... | collective-permute-start | bytes 24584 | tf_op jit(solution)/shard_map/ppermute | solution.py:21
  150.6 3.3 %copy-start.15 = (f32[1,64,5,128]{3,0,2,1:T(1,128)S(1)}, f32[1,64,5,128]{3,0,2,1:T(1,128)}, u32[]{:S(2)}) copy-start(f32[1,64,5,128]{3,0,2,1:T(1,128)} %get-tuple-element.19) | copy-start | bytes 491524
  150.6 3.3 %copy-start.30 = (f32[320]{0:T(512)S(1)}, f32[320]{0:T(512)}, u32[]{:S(2)}) copy-start(f32[320]{0:T(512)} %reshape.286) | copy-start | bytes 3844
  150.6 3.9 %copy-start.21 = (f32[320,32]{0,1:T(8,128)S(1)}, f32[320,32]{0,1:T(8,128)}, u32[]{:S(2)}) copy-start(f32[320,32]{0,1:T(8,128)} %select_reduce_fusion.1) | copy-start | bytes 122884
  150.6 4.5 %copy-start.7 = (f32[4,2,16,512]{3,2,1,0:T(8,128)S(1)}, f32[4,2,16,512]{3,2,1,0:T(8,128)}, u32[]{:S(2)}) copy-start(f32[4,2,16,512]{3,2,1,0:T(8,128)} %copy-done.5) | copy-start | bytes 786436
  150.6 4.5 %copy-start.10 = (bf16[512,128]{1,0:T(8,128)(2,1)S(1)}, bf16[512,128]{1,0:T(8,128)(2,1)}, u32[]{:S(2)}) copy-start(bf16[512,128]{1,0:T(8,128)(2,1)} %param.19) | copy-start | bytes 393220
  150.6 4.5 %copy-start.13 = (f32[4,2,16,512]{3,2,1,0:T(8,128)S(1)}, f32[4,2,16,512]{3,2,1,0:T(8,128)}, u32[]{:S(2)}) copy-start(f32[4,2,16,512]{3,2,1,0:T(8,128)} %copy-done.12) | copy-start | bytes 786436
  150.6 4.5 %copy-start.14 = (f32[4,2,16,512]{3,2,1,0:T(8,128)S(1)}, f32[4,2,16,512]{3,2,1,0:T(8,128)}, u32[]{:S(2)}) copy-start(f32[4,2,16,512]{3,2,1,0:T(8,128)} %get-tuple-element.37) | copy-start | bytes 786436
  150.7 4.5 %copy-start.23 = (bf16[4,2,16,512]{3,2,1,0:T(8,128)(2,1)S(1)}, bf16[4,2,16,512]{3,2,1,0:T(8,128)(2,1)}, u32[]{:S(2)}) copy-start(bf16[4,2,16,512]{3,2,1,0:T(8,128)(2,1)} %copy-done.22) | copy-start | bytes 393220
  150.7 4.5 %copy-start.27 = (f32[4,2,16]{2,1,0:T(2,128)S(1)}, f32[4,2,16]{2,1,0:T(2,128)}, u32[]{:S(2)}) copy-start(f32[4,2,16]{2,1,0:T(2,128)} %get-tuple-element.33) | copy-start | bytes 1540
  153.9 1.5 copy-start.18
  153.9 1.5 copy-start.33
  153.9 1.8 %copy-start.3 = (bf16[512,512]{1,0:T(8,128)(2,1)S(1)}, bf16[512,512]{1,0:T(8,128)(2,1)}, u32[]{:S(2)}) copy-start(bf16[512,512]{1,0:T(8,128)(2,1)} %param.16) | copy-start | bytes 1572868
  155.1 12.0 %copy-start.25 = (f32[512]{0:T(512)S(1)}, f32[512]{0:T(512)}, u32[]{:S(2)}) copy-start(f32[512]{0:T(512)} %param.18) | copy-start | bytes 6148
  155.4 12.1 %copy-start.16 = (bf16[4,2,16,512]{3,2,1,0:T(8,128)(2,1)S(1)}, bf16[4,2,16,512]{3,2,1,0:T(8,128)(2,1)}, u32[]{:S(2)}) copy-start(bf16[4,2,16,512]{3,2,1,0:T(8,128)(2,1)} %param.14) | copy-start | bytes 393220
  155.4 12.1 %copy-start.26 = (f32[4,2,16]{2,1,0:T(2,128)S(1)}, f32[4,2,16]{2,1,0:T(2,128)}, u32[]{:S(2)}) copy-start(f32[4,2,16]{2,1,0:T(2,128)} %get-tuple-element.31) | copy-start | bytes 1540
  155.4 12.1 %copy-start.29 = (f32[512]{0:T(512)S(1)}, f32[512]{0:T(512)}, u32[]{:S(2)}) copy-start(f32[512]{0:T(512)} %param.20) | copy-start | bytes 6148
  156.1 9.5 %collective-permute-start.8 = (bf16[4,2,1,512]{3,2,1,0:T(2,128)(2,1)S(1)}, bf16[4,2,1,512]{3,2,1,0:T(2,128)(2,1)S(1)}, u32[]{:S(2)}, u32[]{:S(2)}) collective-permute-start(bf16[4,2,1,512]{3,2,1,0:T(2,128)(2,1)S(1)} %get-tuple-element.21), channel_id=1, source_target_pairs={{0,1},{1,2},{2,3},{3,4},{4,5},{5,6},{6,7},{7,8},{8,9},{9,10},{10,1... | collective-permute-start | bytes 24584 | tf_op jit(solution)/shard_map/ppermute | solution.py:19
  158.0 8.9 %collective-permute-start.9 = (bf16[4,2,1,512]{3,2,1,0:T(2,128)(2,1)S(1)}, bf16[4,2,1,512]{3,2,1,0:T(2,128)(2,1)S(1)}, u32[]{:S(2)}, u32[]{:S(2)}) collective-permute-start(bf16[4,2,1,512]{3,2,1,0:T(2,128)(2,1)S(1)} %get-tuple-element.22), channel_id=1, source_target_pairs={{1,0},{2,1},{3,2},{4,3},{5,4},{6,5},{7,6},{8,7},{9,8},{10,9},{11,1... | collective-permute-start | bytes 24584 | tf_op jit(solution)/shard_map/ppermute | solution.py:21
where the time goes:
time: 172 us; the launch traced here: 169 us
  starting transfers between devices  90.8 us (53%)
  waiting for transfers between devices  26.7 us (16%)
  other arithmetic  20.5 us (12%)
  local copies, waits for them, and re-layouts  19 us (11%)
  matrix products  11.2 us (7%)
    ppermute x4, starting transfers between devices, padded_2(): lax.ppermute(head, axis, [((i + 1) % count, i) for i in range(count)])  31.3 us
    all_to_all x1, waiting for transfers between devices, per_device(): lax.all_to_all(placed_stencil, 'tile', split_axis=1, concat_axis=1, tiled...  14.7 us
    all_to_all x1, starting transfers between devices, per_device(): lax.all_to_all(placed_stencil, 'tile', split_axis=1, concat_axis=1, tiled...  13.9 us
    ppermute x4, starting transfers between devices, padded_2(): lax.ppermute(tail, axis, [(i, (i + 1) % count) for i in range(count)])  12.4 us
    all_to_all x1, starting transfers between devices, per_device(): lax.all_to_all(bucket_float(report_precision[0]), 'tile', split_axis=1, c...  10 us
    ppermute x2, starting transfers between devices, shifted(): return lax.ppermute(block, axis, route)  9.23 us
    gather x2, local copies, waits for them, and re-layouts, observe(): picked = readout_field[:, arrived_stencil, :]  8.68 us
    all_to_all x1, waiting for transfers between devices, per_device(): lax.all_to_all(bucket_float(report_precision[0]), 'tile', split_axis=1, c...  7.98 us
  transfers between devices with their start and end apart: 14, of which 5 were waited for; matrix products, arithmetic and copies ran while one was open for 20% of the time, Pallas kernels for 0%

commit v1 on v0

v1 whole, which is shorter than its diff:
```python
import functools

import jax
import jax.numpy as jnp
from jax import lax
from jax.experimental import pallas as pl
from jax.experimental.pallas import tpu as pltpu
from jax.sharding import PartitionSpec as P

MESH = pl.DeviceIdType.MESH
CAP = 5
EPSILON = 1e-06
FIELDS = 9
BLOCK = 16
F32 = jnp.float32
BF16 = jnp.bfloat16
HIGHEST = lax.Precision.HIGHEST


def iota(shape, dim):
    return lax.broadcasted_iota(jnp.int32, shape, dim)


def dot(a, b):
    return jnp.dot(a, b, preferred_element_type=F32)


def dot_back(a, b):
    return lax.dot_general(a, b, (((1,), (1,)), ((), ())), preferred_element_type=F32)


def dot_rows(a, b):
    return lax.dot_general(a, b, (((0,), (0,)), ((), ())), preferred_element_type=F32)


def slot_of_lane(lane):
    return lax.shift_right_logical(lane * 57, 9)


def pack_reports(steps, tiles, owner_ref, stencil_ref, weights_ref, values_ref, precision_ref, mt):
    rows = values_ref.shape[1]
    lane = iota((rows, 128), 1)
    row = iota((rows, 128), 0)
    lane_slot = slot_of_lane(lane)
    lane_field = lane - FIELDS * lane_slot
    spread_fields = jnp.where((row == lane_field) & (row < FIELDS), 1.0, 0.0).astype(BF16)
    place = iota((tiles * BLOCK, rows), 0)
    one_hots, operands = [], []
    mt[...] = jnp.zeros_like(mt)
    for k in range(steps):
        owner_row = owner_ref[k]
        mt[k, 0:4, :] = stencil_ref[k].astype(F32)
        mt[k, 4:8, :] = weights_ref[k].astype(F32)
        mt[k, 8:9, :] = precision_ref[0, k : k + 1, :].astype(F32)
        mt[k, 9:10, :] = owner_row.astype(F32)
        columns = mt[k].T
        owner_col = columns[:, 9:10].astype(jnp.int32)
        same = owner_col == owner_row
        rank_row = jnp.sum(jnp.where(same & (row < lane), 1, 0), axis=0, keepdims=True)
        rank_col = jnp.sum(jnp.where(same & (lane < row), 1, 0), axis=1, keepdims=True)
        meta = dot(columns.astype(BF16), spread_fields)
        meta = jnp.where(lane_slot == rank_col + CAP * k, meta, 0.0).astype(BF16)
        base = owner_row * BLOCK
        one_hots.append(jnp.where(place == base + (rank_row + CAP * k), 1.0, 0.0).astype(BF16))
        operands.append(values_ref[k])
        one_hots.append(jnp.where(place == base + CAP * steps, 1.0, 0.0).astype(BF16))
        operands.append(meta)
    return dot(jnp.concatenate(one_hots, axis=1), jnp.concatenate(operands, axis=0)).astype(BF16)


def report_operators(steps, tiles, arrived, cells):
    slots = CAP * steps
    meta = arrived[:, slots, :]
    lane_slot = slot_of_lane(iota((tiles, 128), 1))
    stacked = jnp.concatenate(
        [jnp.where(lane_slot == s, meta, 0.0) for s in range(slots)], axis=0
    ).astype(BF16)
    values = jnp.concatenate([arrived[:, s, :] for s in range(slots)], axis=0)
    lane = iota((128, 384), 0)
    column = iota((128, 384), 1)
    field = lane - FIELDS * slot_of_lane(lane)
    wanted = jnp.minimum(lax.shift_right_logical(column, 5), FIELDS - 1)
    expand = jnp.where((field == wanted) & (lane < FIELDS * slots), 1.0, 0.0).astype(BF16)
    expanded = dot(stacked, expand)
    cell = jnp.bitwise_and(iota((tiles * slots, 128), 1), cells - 1).astype(F32)
    table = jnp.where(expanded[:, 0:128] == cell, expanded[:, 128:256], 0.0)
    precision = expanded[:, 256:384]
    right = jnp.concatenate([precision * table, precision * values], axis=1)
    table = table.astype(BF16)
    high = right.astype(BF16)
    low = (right - high.astype(F32)).astype(BF16)
    r = iota((128, 128), 0)
    c = iota((128, 128), 1)
    fold = jnp.where(jnp.bitwise_and(r, cells - 1) == jnp.bitwise_and(c, cells - 1), 1.0, 0.0)
    member = lax.shift_right_logical(r, 5) == lax.shift_right_logical(c, 5)
    out = []
    for k in range(steps):
        part = slice(k * CAP * tiles, (k + 1) * CAP * tiles)
        both = dot_rows(table[part], high[part]) + dot_rows(table[part], low[part])
        both = jnp.dot(fold, both, precision=HIGHEST, preferred_element_type=F32)
        gram = jnp.dot(both[:, 0:128], fold, precision=HIGHEST, preferred_element_type=F32)
        out.append((jnp.where(member, gram, 0.0), both[:, 128:256]))
    return out


def kernel(
    slots,
    tiles,
    steps,
    control_ref,
    background_ref,
    self_ref,
    neighbour_ref,
    output_ref,
    gain_ref,
    readout_ref,
    error_ref,
    owner_ref,
    stencil_ref,
    weights_ref,
    values_ref,
    precision_ref,
    out_ref,
    mt,
    send_buf,
    recv_buf,
    arrived,
    edge_send,
    edge_recv,
    own,
    west,
    east,
    next_control,
    final_send,
    final_recv,
    report_send_sem,
    report_recv_sem,
    edge_send_sem,
    edge_recv_sem,
    state_send_sem,
    state_recv_sem,
):
    slot = lax.axis_index("slot")
    tile = lax.axis_index("tile")
    east_tile, west_tile = lax.rem(tile + 1, tiles), lax.rem(tile + tiles - 1, tiles)
    next_slot, last_slot = lax.rem(slot + 1, slots), lax.rem(slot + slots - 1, slots)
    rows, channels = control_ref.shape
    groups = rows // BLOCK

    barrier = pltpu.get_barrier_semaphore()

    @pl.loop(1, tiles)
    def _(distance):
        peer = lax.rem(tile + distance, tiles)
        pl.semaphore_signal(barrier, inc=1, device_id=(slot, peer), device_id_type=MESH)

    for peer in (next_slot, last_slot):
        pl.semaphore_signal(barrier, inc=1, device_id=(peer, tile), device_id_type=MESH)

    def edge_copy(turn, side):
        return pltpu.make_async_remote_copy(
            src_ref=edge_send.at[turn, side],
            dst_ref=edge_recv.at[turn, side],
            send_sem=edge_send_sem.at[turn, side],
            recv_sem=edge_recv_sem.at[turn, side],
            device_id=(slot, east_tile if side == 0 else west_tile),
            device_id_type=MESH,
        )

    def set_edges(turn, rounded):
        own[...] = rounded.astype(F32).reshape(groups, BLOCK, channels)
        edge_send[turn, 0] = own[:, BLOCK - 1, :].astype(BF16)
        edge_send[turn, 1] = own[:, 0, :].astype(BF16)

    def send_edges(turn):
        edge_copy(turn, 0).start()
        edge_copy(turn, 1).start()

    def neighbours(turn):
        whole = own[...].reshape(rows, channels)
        west[...] = pltpu.roll(whole, 1, 0).reshape(groups, BLOCK, channels)
        east[...] = pltpu.roll(whole, rows - 1, 0).reshape(groups, BLOCK, channels)
        swapped = jnp.concatenate(
            [whole[BLOCK * (g ^ 1) : BLOCK * (g ^ 1) + BLOCK] for g in range(groups)], axis=0
        )
        edge_copy(turn, 0).wait_recv()
        edge_copy(turn, 1).wait_recv()
        west[:, 0, :] = edge_recv[turn, 0].astype(F32)
        east[:, BLOCK - 1, :] = edge_recv[turn, 1].astype(F32)
        return (
            swapped
            + west[...].reshape(rows, channels)
            + east[...].reshape(rows, channels)
        )

    gain = gain_ref[...]

    def normalize(current):
        inverse_rms = lax.rsqrt(jnp.mean(current * current, axis=-1, keepdims=True) + EPSILON)
        return (current * inverse_rms * gain).astype(BF16), inverse_rms

    control_copy = pltpu.make_async_remote_copy(
        src_ref=control_ref,
        dst_ref=next_control,
        send_sem=state_send_sem.at[0],
        recv_sem=state_recv_sem.at[0],
        device_id=(last_slot, tile),
        device_id_type=MESH,
    )
    final_copy = pltpu.make_async_remote_copy(
        src_ref=final_send,
        dst_ref=final_recv,
        send_sem=state_send_sem.at[1],
        recv_sem=state_recv_sem.at[1],
        device_id=(next_slot, tile),
        device_id_type=MESH,
    )

    current = control_ref[...]
    normed, inverse_rms = normalize(current)
    set_edges(0, normed)
    packed = pack_reports(
        steps, tiles, owner_ref, stencil_ref, weights_ref, values_ref, precision_ref, mt
    )
    send_buf[...] = packed.reshape(tiles, BLOCK, 128)
    pl.semaphore_wait(barrier, tiles + 1)
    send_edges(0)

    @pl.loop(1, tiles)
    def _(distance):
        peer = lax.rem(tile + distance, tiles)
        pltpu.make_async_remote_copy(
            src_ref=send_buf.at[peer],
            dst_ref=recv_buf.at[tile],
            send_sem=report_send_sem,
            recv_sem=report_recv_sem,
            device_id=(slot, peer),
            device_id_type=MESH,
        ).start()

    control_copy.start()
    recv_buf[pl.ds(tile, 1)] = send_buf[pl.ds(tile, 1)]

    states, kept, fields = [], [], []
    for k in range(steps):
        if k > 0:
            normed, inverse_rms = normalize(current)
            set_edges(k, normed)
            send_edges(k)
        linear = dot(normed, self_ref[...])
        mixed = (0.25 * neighbours(k)).astype(BF16)
        linear = linear + dot(mixed, neighbour_ref[...])
        sigmoid = 1.0 / (1.0 + jnp.exp(-linear))
        states.append(current)
        kept.append((inverse_rms, sigmoid * (1.0 + linear * (1.0 - sigmoid))))
        current = current + dot((linear * sigmoid).astype(BF16), output_ref[...])
        fields.append(dot(current.astype(BF16), readout_ref[...]))
    final = current.astype(BF16)
    final_send[...] = final
    final_copy.start()

    others = pl.ds(0, tiles - 1)
    everyone = pltpu.make_async_remote_copy(
        src_ref=send_buf.at[others],
        dst_ref=recv_buf.at[others],
        send_sem=report_send_sem,
        recv_sem=report_recv_sem,
        device_id=(slot, east_tile),
        device_id_type=MESH,
    )
    everyone.wait_recv()
    arrived[...] = recv_buf[...].astype(F32)
    pulls = []
    for (gram, offset), field in zip(report_operators(steps, tiles, arrived, 2 * BLOCK), fields):
        spread = jnp.dot(gram, field, precision=HIGHEST, preferred_element_type=F32) - offset
        pulls.append(dot_back(spread.astype(BF16), readout_ref[...]))

    error = error_ref[...]
    control_copy.wait_recv()
    next_misfit = error * (next_control[...] - final.astype(F32))
    cotangent = pulls[-1] - jnp.where(slot == slots - 1, 0.0, next_misfit)
    for k in reversed(range(steps)):
        turn = 2 * steps - 1 - k
        inverse_rms, slope = kept[k]
        back = dot_back(cotangent.astype(BF16), output_ref[...])
        back = (back * slope).astype(BF16)
        set_edges(turn, dot_back(back, neighbour_ref[...]).astype(BF16))
        send_edges(turn)
        own_part = dot_back(back, self_ref[...])
        scaled = gain * (own_part + 0.25 * neighbours(turn))
        mean = jnp.mean(states[k] * scaled, axis=-1, keepdims=True)
        cubed = inverse_rms * inverse_rms * inverse_rms
        cotangent = cotangent + inverse_rms * scaled - states[k] * (cubed * mean)
        if k > 0:
            cotangent = cotangent + pulls[k - 1]

    final_copy.wait_recv()
    previous = jnp.where(slot == 0, background_ref[...].astype(F32), final_recv[...].astype(F32))
    out_ref[...] = cotangent + error * (control_ref[...] - previous)

    everyone.wait_send()
    for turn in range(2 * steps):
        edge_copy(turn, 0).wait_send()
        edge_copy(turn, 1).wait_send()
    control_copy.wait_send()
    final_copy.wait_send()


def solution(mesh):
    slots, tiles = mesh.shape["slot"], mesh.shape["tile"]

    def per_device(
        control,
        background,
        self_weight,
        neighbour_weight,
        output_weight,
        norm_gain,
        readout,
        error_weight,
        report_owner,
        report_stencil,
        report_weights,
        report_values,
        report_precision,
    ):
        channels = control.shape[-1]
        rows = control.size // channels
        steps = report_values.shape[1]
        groups = rows // BLOCK
        edges = (2 * steps, 2, groups, channels)
        block = (groups, BLOCK, channels)
        message = (tiles, BLOCK, 128)
        out = pl.pallas_call(
            functools.partial(kernel, slots, tiles, steps),
            out_shape=jax.ShapeDtypeStruct((rows, channels), F32),
            in_specs=[pl.BlockSpec(memory_space=pltpu.VMEM)] * 13,
            out_specs=pl.BlockSpec(memory_space=pltpu.VMEM),
            scratch_shapes=[
                pltpu.VMEM((steps, 128, 128), F32),
                pltpu.VMEM(message, BF16),
                pltpu.VMEM(message, BF16),
                pltpu.VMEM(message, F32),
                pltpu.VMEM(edges, BF16),
                pltpu.VMEM(edges, BF16),
                pltpu.VMEM(block, F32),
                pltpu.VMEM(block, F32),
                pltpu.VMEM(block, F32),
                pltpu.VMEM((rows, channels), F32),
                pltpu.VMEM((rows, channels), BF16),
                pltpu.VMEM((rows, channels), BF16),
                pltpu.SemaphoreType.DMA,
                pltpu.SemaphoreType.DMA,
                pltpu.SemaphoreType.DMA((2 * steps, 2)),
                pltpu.SemaphoreType.DMA((2 * steps, 2)),
                pltpu.SemaphoreType.DMA((2,)),
                pltpu.SemaphoreType.DMA((2,)),
            ],
            compiler_params=pltpu.CompilerParams(collective_id=0, has_side_effects=True),
        )(
            control.reshape(rows, channels),
            background.reshape(rows, channels),
            self_weight,
            neighbour_weight,
            output_weight,
            norm_gain.reshape(1, channels),
            readout,
            error_weight.reshape(1, channels),
            report_owner[0].transpose(0, 2, 1),
            report_stencil[0].transpose(0, 2, 1),
            report_weights[0].transpose(0, 2, 1),
            report_values[0],
            report_precision,
        )
        return out.reshape(control.shape)

    in_specs = (
        P("slot", None, None, "tile", None),
        P(None, None, "tile", None),
        P(),
        P(),
        P(),
        P(),
        P(),
        P(),
        P("slot", None, "tile", None),
        P("slot", None, "tile", None),
        P("slot", None, "tile", None),
        P("slot", None, "tile", None),
        P("slot", None, "tile"),
    )
    out_specs = P("slot", None, None, "tile", None)
    return jax.shard_map(
        per_device, mesh=mesh, in_specs=in_specs, out_specs=out_specs, check_vma=False
    )
```

time: 172 us -> 49.2 us (0.29); the launches traced: 169 us -> 49.1 us
  starting transfers between devices: 90.8 us -> 0 us
  Pallas kernels: 0 us -> 47.4 us
  waiting for transfers between devices: 26.7 us -> 0 us
  other arithmetic: 20.5 us -> 0 us
  local copies, waits for them, and re-layouts: 19 us -> 1.67 us
  matrix products: 11.2 us -> 0 us
    ppermute x10 -> x0, starting transfers between devices: 52.9 us -> none  [the longest x4 31.3 us: padded_2(): lax.ppermute(head, axis, [((i + 1) % count, i) for i in range(count)])]
    pallas_call x0 -> x1, Pallas kernels: none -> 47.4 us  [per_device(): pl.pallas_call(functools.partial(kernel, slots, tiles, steps), out_shape=...]
    all_to_all x4 -> x0, starting transfers between devices: 37.9 us -> none  [the longest x1 13.9 us: per_device(): lax.all_to_all(placed_stencil, 'tile', split_axis=1, concat_axis=1, tiled...]
    all_to_all x4 -> x0, waiting for transfers between devices: 22.7 us -> none  [the longest x1 14.7 us: per_device(): lax.all_to_all(placed_stencil, 'tile', split_axis=1, concat_axis=1, tiled...]
    dot_general x22 -> x0, matrix products: 11.2 us -> none  [the longest x8 3.05 us: matmul_back(): lax.dot_general(operand.reshape(-1, operand.shape[-1]), matrix, (((1,), (...]
    reduce_sum x6 -> x0, other arithmetic: 10.1 us -> none  [the longest x2 7.11 us: observe(): predicted = jnp.sum(picked * stencil_weights[None, :, :, None], axis=2)]
    gather x2 -> x0, local copies, waits for them, and re-layouts: 8.68 us -> none  [observe(): picked = readout_field[:, arrived_stencil, :]]
    convert_element_type x9 -> x0, other arithmetic: 4.58 us -> none  [the longest x1 1.95 us: observe(): targets = arrived_values.astype(jnp.float32)[None]]
  transfers between devices with their start and end apart: 14 -> 0, of which waited for: 5 -> 0; matrix products, arithmetic and copies ran while one was open for 20% -> 0% of each run, Pallas kernels for 0% -> 0%
where the time goes in v1:
time: 49.2 us; the launch traced here: 49.1 us
  Pallas kernels  47.4 us (96%)
  local copies, waits for them, and re-layouts  1.67 us (3%)
    pallas_call x1, Pallas kernels, per_device(): pl.pallas_call(functools.partial(kernel, slots, tiles, steps), out_shape=...  47.4 us
    unnamed x1, local copies, waits for them, and re-layouts  1.67 us

profile of v1, /device:TPU:6, one launch (start us, length us, event | category | flops | bytes accessed | tf_op | source)
XLA Modules:
  0.0 49.1 jit_solution(3327212436825108573)
XLA Ops:
  0.0 47.4 %shard_map.127 = f32[128,512]{1,0:T(8,128)} custom-call(f32[128,512]{1,0:T(8,128)} %bitcast.14, bf16[128,512]{1,0:T(8,128)(2,1)} %bitcast.15, bf16[512,512]{1,0:T(8,128)(2,1)} %self_ref.1, bf16[512,512]{1,0:T(8,128)(2,1)} %neighbour_ref.1, bf16[512,512]{1,0:T(8,128)(2,1)} %output_ref.1, f32[1,512]{1,0:T(1,128)} %bitcast.18, bf16[512,128]{1,0:T(8,128)(2,1)} %readout_ref.1, ...), custom_call_target="tpu_custom_call" | custom-call | tf_op jit(solution)/shard_map/pallas_call | solution.py:334
  47.4 1.7 %copy.15 = f32[1,4,2,16,512]{4,3,2,1,0:T(8,128)} copy(f32[1,4,2,16,512]{4,3,2,1,0:T(8,128)} %bitcast.13) | data formatting | bytes 524288

commit v2 on v1

--- a/solution.py
+++ b/solution.py
@@ -12,6 +12,7 @@
 EPSILON = 1e-06
 FIELDS = 9
 BLOCK = 16
+SENT = 12
 F32 = jnp.float32
 BF16 = jnp.bfloat16
 HIGHEST = lax.Precision.HIGHEST
@@ -35,6 +36,24 @@
 
 def slot_of_lane(lane):
     return lax.shift_right_logical(lane * 57, 9)
+
+
+def farthest_first(tile, tiles, ring, send):
+    outer = tiles // ring
+    line, place = tile // ring, lax.rem(tile, ring)
+
+    def one(turn, across):
+        step = (turn + 1) // 2
+        along = jnp.where(lax.rem(turn, 2) == 1, ring // 2 + step, ring // 2 - step)
+        send(lax.rem(line + across, outer) * ring + lax.rem(place + along, ring))
+
+    @pl.loop(0, ring - 1)
+    def _(turn):
+        for across in range(outer):
+            one(turn, (across + outer // 2) % outer)
+
+    for across in range(1, outer):
+        send(lax.rem(line + across, outer) * ring + place)
 
 
 def pack_reports(steps, tiles, owner_ref, stencil_ref, weights_ref, values_ref, precision_ref, mt):
@@ -106,7 +125,22 @@
 def kernel(
     slots,
     tiles,
+    ring,
     steps,
+    control_hbm,
+    background_hbm,
+    self_hbm,
+    neighbour_hbm,
+    output_hbm,
+    gain_hbm,
+    readout_hbm,
+    error_hbm,
+    owner_hbm,
+    stencil_hbm,
+    weights_hbm,
+    values_hbm,
+    precision_hbm,
+    out_ref,
     control_ref,
     background_ref,
     self_ref,
@@ -120,7 +154,7 @@
     weights_ref,
     values_ref,
     precision_ref,
-    out_ref,
+    fetch_sem,
     mt,
     send_buf,
     recv_buf,
@@ -147,15 +181,37 @@
     rows, channels = control_ref.shape
     groups = rows // BLOCK
 
+    fetches = [
+        pltpu.make_async_copy(source, target, fetch_sem.at[i])
+        for i, (source, target) in enumerate(
+            (
+                (control_hbm, control_ref),
+                (gain_hbm, gain_ref),
+                (owner_hbm, owner_ref),
+                (stencil_hbm, stencil_ref),
+                (weights_hbm, weights_ref),
+                (precision_hbm, precision_ref),
+                (values_hbm, values_ref),
+                (self_hbm, self_ref),
+                (neighbour_hbm, neighbour_ref),
+                (output_hbm, output_ref),
+                (readout_hbm, readout_ref),
+                (error_hbm, error_ref),
+                (background_hbm, background_ref),
+            )
+        )
+    ]
     barrier = pltpu.get_barrier_semaphore()
 
-    @pl.loop(1, tiles)
-    def _(distance):
-        peer = lax.rem(tile + distance, tiles)
+    def greet(peer):
         pl.semaphore_signal(barrier, inc=1, device_id=(slot, peer), device_id_type=MESH)
 
+    farthest_first(tile, tiles, ring, greet)
     for peer in (next_slot, last_slot):
         pl.semaphore_signal(barrier, inc=1, device_id=(peer, tile), device_id_type=MESH)
+
+    for fetch in fetches:
+        fetch.start()
 
     def edge_copy(turn, side):
         return pltpu.make_async_remote_copy(
@@ -193,6 +249,8 @@
             + east[...].reshape(rows, channels)
         )
 
+    for fetch in fetches:
+        fetch.wait()
     gain = gain_ref[...]
 
     def normalize(current):
@@ -226,18 +284,17 @@
     pl.semaphore_wait(barrier, tiles + 1)
     send_edges(0)
 
-    @pl.loop(1, tiles)
-    def _(distance):
-        peer = lax.rem(tile + distance, tiles)
+    def send_reports(peer):
         pltpu.make_async_remote_copy(
-            src_ref=send_buf.at[peer],
-            dst_ref=recv_buf.at[tile],
+            src_ref=send_buf.at[peer, 0:SENT],
+            dst_ref=recv_buf.at[tile, 0:SENT],
             send_sem=report_send_sem,
             recv_sem=report_recv_sem,
             device_id=(slot, peer),
             device_id_type=MESH,
         ).start()
 
+    farthest_first(tile, tiles, ring, send_reports)
     control_copy.start()
     recv_buf[pl.ds(tile, 1)] = send_buf[pl.ds(tile, 1)]
 
@@ -261,8 +318,8 @@
 
     others = pl.ds(0, tiles - 1)
     everyone = pltpu.make_async_remote_copy(
-        src_ref=send_buf.at[others],
-        dst_ref=recv_buf.at[others],
+        src_ref=send_buf.at[others, 0:SENT],
+        dst_ref=recv_buf.at[others, 0:SENT],
         send_sem=report_send_sem,
         recv_sem=report_recv_sem,
         device_id=(slot, east_tile),
@@ -328,15 +385,33 @@
         rows = control.size // channels
         steps = report_values.shape[1]
         groups = rows // BLOCK
+        ring = 16 if tiles % 16 == 0 else tiles
         edges = (2 * steps, 2, groups, channels)
         block = (groups, BLOCK, channels)
         message = (tiles, BLOCK, 128)
+        operands = (
+            control.reshape(rows, channels),
+            background.reshape(rows, channels),
+            self_weight,
+            neighbour_weight,
+            output_weight,
+            norm_gain.reshape(1, channels),
+            readout,
+            error_weight.reshape(1, channels),
+            report_owner[0].transpose(0, 2, 1),
+            report_stencil[0].transpose(0, 2, 1),
+            report_weights[0].transpose(0, 2, 1),
+            report_values[0],
+            report_precision,
+        )
         out = pl.pallas_call(
-            functools.partial(kernel, slots, tiles, steps),
+            functools.partial(kernel, slots, tiles, ring, steps),
             out_shape=jax.ShapeDtypeStruct((rows, channels), F32),
-            in_specs=[pl.BlockSpec(memory_space=pltpu.VMEM)] * 13,
+            in_specs=[pl.BlockSpec(memory_space=pl.ANY)] * len(operands),
             out_specs=pl.BlockSpec(memory_space=pltpu.VMEM),
             scratch_shapes=[
+                *[pltpu.VMEM(operand.shape, operand.dtype) for operand in operands],
+                pltpu.SemaphoreType.DMA((len(operands),)),
                 pltpu.VMEM((steps, 128, 128), F32),
                 pltpu.VMEM(message, BF16),
                 pltpu.VMEM(message, BF16),
@@ -357,21 +432,7 @@
                 pltpu.SemaphoreType.DMA((2,)),
             ],
             compiler_params=pltpu.CompilerParams(collective_id=0, has_side_effects=True),
-        )(
-            control.reshape(rows, channels),
-            background.reshape(rows, channels),
-            self_weight,
-            neighbour_weight,
-            output_weight,
-            norm_gain.reshape(1, channels),
-            readout,
-            error_weight.reshape(1, channels),
-            report_owner[0].transpose(0, 2, 1),
-            report_stencil[0].transpose(0, 2, 1),
-            report_weights[0].transpose(0, 2, 1),
-            report_values[0],
-            report_precision,
-        )
+        )(*operands)
         return out.reshape(control.shape)
 
     in_specs = (

time: 49.2 us -> 44.8 us (0.911)
  Pallas kernels: 47.4 us -> 43 us
    pallas_call x1, Pallas kernels: 47.4 us -> 43 us  [per_device(): pl.pallas_call(functools.partial(kernel, slots, tiles, ring, steps), out_...]
where the time goes in v2:
time: 44.8 us; the launch traced here: 44.6 us
  Pallas kernels  43 us (96%)
  local copies, waits for them, and re-layouts  1.67 us (4%)
    pallas_call x1, Pallas kernels, per_device(): pl.pallas_call(functools.partial(kernel, slots, tiles, ring, steps), out_...  43 us
    unnamed x1, local copies, waits for them, and re-layouts  1.67 us

profile of v2, /device:TPU:6, one launch (start us, length us, event | category | flops | bytes accessed | tf_op | source)
XLA Modules:
  0.0 44.6 jit_solution(1817554973728067213)
XLA Ops:
  0.0 43.0 %shard_map.127 = f32[128,512]{1,0:T(8,128)} custom-call(f32[128,512]{1,0:T(8,128)} %bitcast.14, bf16[128,512]{1,0:T(8,128)(2,1)} %bitcast.15, bf16[512,512]{1,0:T(8,128)(2,1)} %self_hbm.1, bf16[512,512]{1,0:T(8,128)(2,1)} %neighbour_hbm.1, bf16[512,512]{1,0:T(8,128)(2,1)} %output_hbm.1, f32[1,512]{1,0:T(1,128)} %bitcast.18, bf16[512,128]{1,0:T(8,128)(2,1)} %readout_hbm.1, ...), custom_call_target="tpu_custom_call" | custom-call | tf_op jit(solution)/shard_map/pallas_call | solution.py:407
  43.0 1.7 %copy.15 = f32[1,4,2,16,512]{4,3,2,1,0:T(8,128)} copy(f32[1,4,2,16,512]{4,3,2,1,0:T(8,128)} %bitcast.13) | data formatting | bytes 524288

commit v3 on v2

--- a/solution.py
+++ b/solution.py
@@ -173,6 +173,13 @@
     edge_recv_sem,
     state_send_sem,
     state_recv_sem,
+    wide_send,
+    wide_recv,
+    spread_send,
+    spread_recv,
+    wide_spread,
+    side_send_sem,
+    side_recv_sem,
 ):
     slot = lax.axis_index("slot")
     tile = lax.axis_index("tile")
@@ -232,17 +239,21 @@
         edge_copy(turn, 0).start()
         edge_copy(turn, 1).start()
 
-    def neighbours(turn):
+    def shift_rows():
         whole = own[...].reshape(rows, channels)
         west[...] = pltpu.roll(whole, 1, 0).reshape(groups, BLOCK, channels)
         east[...] = pltpu.roll(whole, rows - 1, 0).reshape(groups, BLOCK, channels)
+
+    def neighbours(turn=None, halo=None):
+        whole = own[...].reshape(rows, channels)
         swapped = jnp.concatenate(
             [whole[BLOCK * (g ^ 1) : BLOCK * (g ^ 1) + BLOCK] for g in range(groups)], axis=0
         )
-        edge_copy(turn, 0).wait_recv()
-        edge_copy(turn, 1).wait_recv()
-        west[:, 0, :] = edge_recv[turn, 0].astype(F32)
-        east[:, BLOCK - 1, :] = edge_recv[turn, 1].astype(F32)
+        if halo is None:
+            edge_copy(turn, 0).wait_recv()
+            edge_copy(turn, 1).wait_recv()
+            halo = edge_recv[turn, 0].astype(F32), edge_recv[turn, 1].astype(F32)
+        west[:, 0, :], east[:, BLOCK - 1, :] = halo
         return (
             swapped
             + west[...].reshape(rows, channels)
@@ -251,6 +262,37 @@
 
     for fetch in fetches:
         fetch.wait()
+    def side_copy(source, target, index, side):
+        return pltpu.make_async_remote_copy(
+            src_ref=source.at[side],
+            dst_ref=target.at[side],
+            send_sem=side_send_sem.at[index, side],
+            recv_sem=side_recv_sem.at[index, side],
+            device_id=(slot, east_tile if side == 0 else west_tile),
+            device_id_type=MESH,
+        )
+
+    side_copies = [
+        side_copy(source, target, index, side)
+        for index, (source, target) in enumerate(
+            ((wide_send, wide_recv), (spread_send, spread_recv))
+        )
+        for side in range(2)
+    ]
+
+    def border(scratch, value, depth):
+        scratch[...] = value.reshape(scratch.shape)
+        return [
+            [scratch[:, BLOCK - 1 - d, :] for d in range(depth)],
+            [scratch[:, d, :] for d in range(depth)],
+        ]
+
+    def send_borders(buffer, first_copy, parts):
+        for side in range(2):
+            flat = [piece for part in parts for piece in part[side]]
+            buffer[side] = jnp.concatenate(flat, axis=0).astype(BF16)
+            side_copies[first_copy + side].start()
+
     gain = gain_ref[...]
 
     def normalize(current):
@@ -305,6 +347,7 @@
             set_edges(k, normed)
             send_edges(k)
         linear = dot(normed, self_ref[...])
+        shift_rows()
         mixed = (0.25 * neighbours(k)).astype(BF16)
         linear = linear + dot(mixed, neighbour_ref[...])
         sigmoid = 1.0 / (1.0 + jnp.exp(-linear))
@@ -316,6 +359,21 @@
     final_send[...] = final
     final_copy.start()
 
+    error = error_ref[...]
+    control_copy.wait_recv()
+    next_misfit = error * (next_control[...] - final.astype(F32))
+    next_misfit = jnp.where(slot == slots - 1, 0.0, next_misfit)
+    send_borders(
+        wide_send,
+        0,
+        [
+            border(own, kept[1][1], 2),
+            border(west, next_misfit, 2),
+            border(east, kept[0][1], 1),
+            border(own, states[1], 1),
+        ],
+    )
+
     others = pl.ds(0, tiles - 1)
     everyone = pltpu.make_async_remote_copy(
         src_ref=send_buf.at[others, 0:SENT],
@@ -327,36 +385,92 @@
     )
     everyone.wait_recv()
     arrived[...] = recv_buf[...].astype(F32)
-    pulls = []
+    spreads, pulls = [], []
     for (gram, offset), field in zip(report_operators(steps, tiles, arrived, 2 * BLOCK), fields):
         spread = jnp.dot(gram, field, precision=HIGHEST, preferred_element_type=F32) - offset
-        pulls.append(dot_back(spread.astype(BF16), readout_ref[...]))
-
-    error = error_ref[...]
-    control_copy.wait_recv()
-    next_misfit = error * (next_control[...] - final.astype(F32))
-    cotangent = pulls[-1] - jnp.where(slot == slots - 1, 0.0, next_misfit)
-    for k in reversed(range(steps)):
-        turn = 2 * steps - 1 - k
-        inverse_rms, slope = kept[k]
-        back = dot_back(cotangent.astype(BF16), output_ref[...])
-        back = (back * slope).astype(BF16)
-        set_edges(turn, dot_back(back, neighbour_ref[...]).astype(BF16))
-        send_edges(turn)
-        own_part = dot_back(back, self_ref[...])
-        scaled = gain * (own_part + 0.25 * neighbours(turn))
-        mean = jnp.mean(states[k] * scaled, axis=-1, keepdims=True)
+        spreads.append(spread.astype(BF16))
+    send_borders(
+        spread_send,
+        2,
+        [
+            border(wide_spread, spreads[1].astype(F32), 2),
+            border(wide_spread, spreads[0].astype(F32), 1),
+        ],
+    )
+    for spread in spreads:
+        pulls.append(dot_back(spread, readout_ref[...]))
+    cotangent = pulls[1] - next_misfit
+
+    def beyond(buffer, index):
+        piece = slice(groups * index, groups * (index + 1))
+        return [buffer[side].astype(F32)[piece] for side in range(2)]
+
+    side_copies[0].wait_recv()
+    side_copies[1].wait_recv()
+    wide_slope = jnp.concatenate(beyond(wide_recv, 0) + beyond(wide_recv, 1), axis=0)
+    wide_misfit = jnp.concatenate(beyond(wide_recv, 2) + beyond(wide_recv, 3), axis=0)
+    wide_slope_0 = jnp.concatenate(beyond(wide_recv, 4), axis=0)
+    wide_state = jnp.concatenate(beyond(wide_recv, 5), axis=0)
+    side_copies[2].wait_recv()
+    side_copies[3].wait_recv()
+    wide_pull = dot_back(
+        jnp.concatenate(
+            beyond(spread_recv, 0) + beyond(spread_recv, 1) + beyond(spread_recv, 2), axis=0
+        ).astype(BF16),
+        readout_ref[...],
+    )
+    close = 2 * groups
+    wide = wide_pull[0 : 2 * close] - wide_misfit
+
+    def pulled_back(inner, outer, inner_slope, outer_slope):
+        both = jnp.concatenate([inner, outer], axis=0).astype(BF16)
+        slope = jnp.concatenate([inner_slope, outer_slope], axis=0)
+        back = (dot_back(both, output_ref[...]) * slope).astype(BF16)
+        mixed = dot_back(back, neighbour_ref[...]).astype(BF16).astype(F32)
+        own[...] = mixed[0:rows].reshape(groups, BLOCK, channels)
+        shift_rows()
+        return dot_back(back, self_ref[...]), mixed[rows:]
+
+    def adjoint(state, inverse_rms, cotangent, grad_normed):
+        scaled = gain * grad_normed
+        mean = jnp.mean(state * scaled, axis=-1, keepdims=True)
         cubed = inverse_rms * inverse_rms * inverse_rms
-        cotangent = cotangent + inverse_rms * scaled - states[k] * (cubed * mean)
-        if k > 0:
-            cotangent = cotangent + pulls[k - 1]
+        return cotangent + inverse_rms * scaled - state * (cubed * mean)
+
+    direct, mixed = pulled_back(cotangent, wide, kept[1][1], wide_slope)
+    halo = mixed[0:groups], mixed[groups:close]
+    even = lax.rem(iota((close, channels), 0), 2) == 0
+    beside = jnp.where(
+        even, pltpu.roll(mixed[0:close], close - 1, 0), pltpu.roll(mixed[0:close], 1, 0)
+    )
+    beside = beside + mixed[close:]
+    beside = beside + jnp.concatenate([own[:, 0, :], own[:, BLOCK - 1, :]], axis=0)
+    wide = adjoint(
+        wide_state,
+        lax.rsqrt(jnp.mean(wide_state * wide_state, axis=-1, keepdims=True) + EPSILON),
+        wide[0:close],
+        direct[rows : rows + close] + 0.25 * beside,
+    )
+    wide = wide + wide_pull[2 * close :]
+    cotangent = adjoint(
+        states[1], kept[1][0], cotangent, direct[0:rows] + 0.25 * neighbours(halo=halo)
+    )
+    cotangent = cotangent + pulls[0]
+
+    direct, mixed = pulled_back(cotangent, wide, kept[0][1], wide_slope_0)
+    halo = mixed[0:groups], mixed[groups:close]
+    cotangent = adjoint(
+        states[0], kept[0][0], cotangent, direct[0:rows] + 0.25 * neighbours(halo=halo)
+    )
 
     final_copy.wait_recv()
     previous = jnp.where(slot == 0, background_ref[...].astype(F32), final_recv[...].astype(F32))
     out_ref[...] = cotangent + error * (control_ref[...] - previous)
 
     everyone.wait_send()
-    for turn in range(2 * steps):
+    for copy in side_copies:
+        copy.wait_send()
+    for turn in range(steps):
         edge_copy(turn, 0).wait_send()
         edge_copy(turn, 1).wait_send()
     control_copy.wait_send()
@@ -386,7 +500,7 @@
         steps = report_values.shape[1]
         groups = rows // BLOCK
         ring = 16 if tiles % 16 == 0 else tiles
-        edges = (2 * steps, 2, groups, channels)
+        edges = (steps, 2, groups, channels)
         block = (groups, BLOCK, channels)
         message = (tiles, BLOCK, 128)
         operands = (
@@ -426,10 +540,17 @@
                 pltpu.VMEM((rows, channels), BF16),
                 pltpu.SemaphoreType.DMA,
                 pltpu.SemaphoreType.DMA,
-                pltpu.SemaphoreType.DMA((2 * steps, 2)),
-                pltpu.SemaphoreType.DMA((2 * steps, 2)),
+                pltpu.SemaphoreType.DMA((steps, 2)),
+                pltpu.SemaphoreType.DMA((steps, 2)),
                 pltpu.SemaphoreType.DMA((2,)),
                 pltpu.SemaphoreType.DMA((2,)),
+                pltpu.VMEM((2, 6 * groups, channels), BF16),
+                pltpu.VMEM((2, 6 * groups, channels), BF16),
+                pltpu.VMEM((2, 3 * groups, 128), BF16),
+                pltpu.VMEM((2, 3 * groups, 128), BF16),
+                pltpu.VMEM((groups, BLOCK, 128), F32),
+                pltpu.SemaphoreType.DMA((2, 2)),
+                pltpu.SemaphoreType.DMA((2, 2)),
             ],
             compiler_params=pltpu.CompilerParams(collective_id=0, has_side_effects=True),
         )(*operands)

time: 44.8 us -> 40.6 us (0.906)
  Pallas kernels: 43 us -> 38.8 us
    pallas_call x1, Pallas kernels: 43 us -> 38.8 us  [per_device(): pl.pallas_call(functools.partial(kernel, slots, tiles, ring, steps), out_...]
where the time goes in v3:
time: 40.6 us; the launch traced here: 40.5 us
  Pallas kernels  38.8 us (96%)
  local copies, waits for them, and re-layouts  1.67 us (4%)
    pallas_call x1, Pallas kernels, per_device(): pl.pallas_call(functools.partial(kernel, slots, tiles, ring, steps), out_...  38.8 us
    unnamed x1, local copies, waits for them, and re-layouts  1.67 us

profile of v3, /device:TPU:6, one launch (start us, length us, event | category | flops | bytes accessed | tf_op | source)
XLA Modules:
  0.0 40.5 jit_solution(2349712421298326857)
XLA Ops:
  0.0 38.8 %shard_map.127 = f32[128,512]{1,0:T(8,128)} custom-call(f32[128,512]{1,0:T(8,128)} %bitcast.14, bf16[128,512]{1,0:T(8,128)(2,1)} %bitcast.15, bf16[512,512]{1,0:T(8,128)(2,1)} %self_hbm.1, bf16[512,512]{1,0:T(8,128)(2,1)} %neighbour_hbm.1, bf16[512,512]{1,0:T(8,128)(2,1)} %output_hbm.1, f32[1,512]{1,0:T(1,128)} %bitcast.18, bf16[512,128]{1,0:T(8,128)(2,1)} %readout_hbm.1, ...), custom_call_target="tpu_custom_call" | custom-call | tf_op jit(solution)/shard_map/pallas_call | solution.py:521
  38.8 1.7 %copy.15 = f32[1,4,2,16,512]{4,3,2,1,0:T(8,128)} copy(f32[1,4,2,16,512]{4,3,2,1,0:T(8,128)} %bitcast.13) | data formatting | bytes 524288

commit v4 on v3

--- a/solution.py
+++ b/solution.py
@@ -175,6 +175,8 @@
     state_recv_sem,
     wide_send,
     wide_recv,
+    late_send,
+    late_recv,
     spread_send,
     spread_recv,
     wide_spread,
@@ -275,7 +277,7 @@
     side_copies = [
         side_copy(source, target, index, side)
         for index, (source, target) in enumerate(
-            ((wide_send, wide_recv), (spread_send, spread_recv))
+            ((wide_send, wide_recv), (spread_send, spread_recv), (late_send, late_recv))
         )
         for side in range(2)
     ]
@@ -353,6 +355,16 @@
         sigmoid = 1.0 / (1.0 + jnp.exp(-linear))
         states.append(current)
         kept.append((inverse_rms, sigmoid * (1.0 + linear * (1.0 - sigmoid))))
+        if k == 1:
+            send_borders(
+                wide_send,
+                0,
+                [
+                    border(own, kept[1][1], 2),
+                    border(east, kept[0][1], 1),
+                    border(own, states[1], 1),
+                ],
+            )
         current = current + dot((linear * sigmoid).astype(BF16), output_ref[...])
         fields.append(dot(current.astype(BF16), readout_ref[...]))
     final = current.astype(BF16)
@@ -363,16 +375,7 @@
     control_copy.wait_recv()
     next_misfit = error * (next_control[...] - final.astype(F32))
     next_misfit = jnp.where(slot == slots - 1, 0.0, next_misfit)
-    send_borders(
-        wide_send,
-        0,
-        [
-            border(own, kept[1][1], 2),
-            border(west, next_misfit, 2),
-            border(east, kept[0][1], 1),
-            border(own, states[1], 1),
-        ],
-    )
+    send_borders(late_send, 4, [border(west, next_misfit, 2)])
 
     others = pl.ds(0, tiles - 1)
     everyone = pltpu.make_async_remote_copy(
@@ -407,10 +410,12 @@
 
     side_copies[0].wait_recv()
     side_copies[1].wait_recv()
+    side_copies[4].wait_recv()
+    side_copies[5].wait_recv()
     wide_slope = jnp.concatenate(beyond(wide_recv, 0) + beyond(wide_recv, 1), axis=0)
-    wide_misfit = jnp.concatenate(beyond(wide_recv, 2) + beyond(wide_recv, 3), axis=0)
-    wide_slope_0 = jnp.concatenate(beyond(wide_recv, 4), axis=0)
-    wide_state = jnp.concatenate(beyond(wide_recv, 5), axis=0)
+    wide_misfit = jnp.concatenate(beyond(late_recv, 0) + beyond(late_recv, 1), axis=0)
+    wide_slope_0 = jnp.concatenate(beyond(wide_recv, 2), axis=0)
+    wide_state = jnp.concatenate(beyond(wide_recv, 3), axis=0)
     side_copies[2].wait_recv()
     side_copies[3].wait_recv()
     wide_pull = dot_back(
@@ -544,13 +549,15 @@
                 pltpu.SemaphoreType.DMA((steps, 2)),
                 pltpu.SemaphoreType.DMA((2,)),
                 pltpu.SemaphoreType.DMA((2,)),
-                pltpu.VMEM((2, 6 * groups, channels), BF16),
-                pltpu.VMEM((2, 6 * groups, channels), BF16),
+                pltpu.VMEM((2, 4 * groups, channels), BF16),
+                pltpu.VMEM((2, 4 * groups, channels), BF16),
+                pltpu.VMEM((2, 2 * groups, channels), BF16),
+                pltpu.VMEM((2, 2 * groups, channels), BF16),
                 pltpu.VMEM((2, 3 * groups, 128), BF16),
                 pltpu.VMEM((2, 3 * groups, 128), BF16),
                 pltpu.VMEM((groups, BLOCK, 128), F32),
-                pltpu.SemaphoreType.DMA((2, 2)),
-                pltpu.SemaphoreType.DMA((2, 2)),
+                pltpu.SemaphoreType.DMA((3, 2)),
+                pltpu.SemaphoreType.DMA((3, 2)),
             ],
             compiler_params=pltpu.CompilerParams(collective_id=0, has_side_effects=True),
         )(*operands)

time: 40.6 us -> 40.7 us (level)
  no operation moved by 1% of the time
where the time goes in v4:
time: 40.7 us; the launch traced here: 40.5 us
  Pallas kernels  38.9 us (96%)
  local copies, waits for them, and re-layouts  1.67 us (4%)
    pallas_call x1, Pallas kernels, per_device(): pl.pallas_call(functools.partial(kernel, slots, tiles, ring, steps), out_...  38.9 us
    unnamed x1, local copies, waits for them, and re-layouts  1.67 us

profile of v4, /device:TPU:6, one launch (start us, length us, event | category | flops | bytes accessed | tf_op | source)
XLA Modules:
  0.0 40.5 jit_solution(18118510207752096595)
XLA Ops:
  0.0 38.9 %shard_map.127 = f32[128,512]{1,0:T(8,128)} custom-call(f32[128,512]{1,0:T(8,128)} %bitcast.14, bf16[128,512]{1,0:T(8,128)(2,1)} %bitcast.15, bf16[512,512]{1,0:T(8,128)(2,1)} %self_hbm.1, bf16[512,512]{1,0:T(8,128)(2,1)} %neighbour_hbm.1, bf16[512,512]{1,0:T(8,128)(2,1)} %output_hbm.1, f32[1,512]{1,0:T(1,128)} %bitcast.18, bf16[512,128]{1,0:T(8,128)(2,1)} %readout_hbm.1, ...), custom_call_target="tpu_custom_call" | custom-call | tf_op jit(solution)/shard_map/pallas_call | solution.py:526
  38.9 1.7 %copy.15 = f32[1,4,2,16,512]{4,3,2,1,0:T(8,128)} copy(f32[1,4,2,16,512]{4,3,2,1,0:T(8,128)} %bitcast.13) | data formatting | bytes 524288
